TPU v7x, 32 devices: a whole 2x2x4 slice. The times are simulated.
32 devices in a mesh: atom: 8 (over z, core), kvec: 4 (over y, x).
Axes of the slice: x: 2, y: 2, z: 4, core: 2. Of those that a mesh axis runs over, the one named last changes fastest.
Arguments:
- features: float32 [12288, 256], P(('atom', 'kvec')), may hold values from -6 to 6
- fractions: int32 [3, 12288], P(None, 'atom'), may hold values from 0 to 1023
- wave_index: int32 [3, 2048], P(None, 'kvec'), may hold values from -12 to 12
- brick_count: int32 [8], replicated, may hold values from 1 to 1536, 6144 in all
- value_weight: float32 [256, 256], replicated, may hold values from -0.375 to 0.375
- k_filter: float32 [2, 2048, 256], P(None, 'kvec'), may hold values from -6 to 6
- mix_weight: float32 [2, 256, 256], replicated, may hold values from -0.25 to 0.25
- out_weight: float32 [256, 256], replicated, may hold values from -0.375 to 0.375
- norm_gain: float32 [256], replicated, may hold values from 0.5 to 1.5
- up_weight: float32 [256, 512], replicated, may hold values from -0.375 to 0.375
- down_weight: float32 [512, 256], replicated, may hold values from -0.25 to 0.25
Outputs:
- updated: float32 [12288, 256], P(('atom', 'kvec'))
Inputs may be any that keep to these rules, and one draw needn't show every extreme that they name: Brick b holds its atoms in its first brick_count[b] slots; the counts sum to 6144 and the largest equals 1536.
All inputs are finite; a program needn't handle non-finite values.
Results may differ from a plain program's by a relative error of at most 0.0003.
Values sent between devices are 32-bit elements; how exact they have to be, the bound alone decides.
A program may use at most 64 MiB of HBM per device.

v0:
```python
import math

import jax
import jax.numpy as jnp
from jax import lax
from jax.sharding import PartitionSpec as P

phase_step = 2.0 * math.pi / 1024.0
exact = lax.Precision.HIGHEST


def phases(frac_rows, wave_index):
    phase_index = frac_rows[0][:, None] * wave_index[0][None, :]
    phase_index = phase_index + frac_rows[1][:, None] * wave_index[1][None, :]
    phase_index = phase_index + frac_rows[2][:, None] * wave_index[2][None, :]
    angles = jnp.mod(phase_index, 1024).astype(jnp.float32) * phase_step
    return (jnp.cos(angles), jnp.sin(angles))


def mixing(real_part, imag_part, filt_real, filt_imag, mix_weight, normalizer):
    mixed_real = real_part * filt_real - imag_part * filt_imag
    mixed_imag = real_part * filt_imag + imag_part * filt_real
    out_real = (
        jnp.dot(mixed_real, mix_weight[0], precision=exact)
        - jnp.dot(mixed_imag, mix_weight[1], precision=exact)
    ) * normalizer
    out_imag = (
        jnp.dot(mixed_real, mix_weight[1], precision=exact)
        + jnp.dot(mixed_imag, mix_weight[0], precision=exact)
    ) * normalizer
    return (out_real, out_imag)


def shards(
    features,
    fractions,
    wave_index,
    brick_count,
    value_weight,
    k_filter,
    mix_weight,
    out_weight,
    norm_gain,
    up_weight,
    down_weight,
):
    share_rows = features.shape[0]
    feat_width = features.shape[1]
    groups = lax.axis_size("kvec")
    bricks = lax.axis_size("atom")
    capacity = share_rows * groups
    k_shard = wave_index.shape[1]
    normalizer = 1.0 / math.sqrt(bricks * capacity // 2 * (k_shard * groups))
    own_brick = lax.axis_index("atom")
    own_group = lax.axis_index("kvec")
    brick_ids = jnp.arange(bricks, dtype=jnp.int32)
    brick_live = jnp.sum(jnp.where(brick_ids == own_brick, brick_count, 0))
    row_offset = own_group * share_rows
    local_slots = row_offset + jnp.arange(share_rows, dtype=jnp.int32)
    live_mask = (local_slots < brick_live).astype(jnp.float32)
    projected = jnp.dot(features, value_weight, precision=exact) * live_mask[:, None]
    contract = (((0,), (0,)), ((), ()))
    values = lax.all_gather(projected, "kvec", axis=0, tiled=True)
    block_rows = math.gcd(capacity, 512)

    def accumulate(counter, partial_value):
        begin = counter * block_rows
        value_rows = lax.dynamic_slice_in_dim(values, begin, block_rows, 0)
        cosine, sine_part = phases(
            lax.dynamic_slice_in_dim(fractions, begin, block_rows, 1), wave_index
        )
        real_part = partial_value[0] + lax.dot_general(
            cosine, value_rows, contract, precision=exact
        )
        imag_part = partial_value[1] - lax.dot_general(
            sine_part, value_rows, contract, precision=exact
        )
        return (real_part, imag_part)

    block_count = (brick_live + block_rows - 1) // block_rows
    empty_sums = jnp.zeros((k_shard, feat_width), jnp.float32)
    real_sf, imag_sf = lax.fori_loop(0, block_count, accumulate, (empty_sums, empty_sums))
    real_sf, imag_sf = lax.psum((real_sf, imag_sf), "atom")
    filt_real, filt_imag = mixing(
        real_sf, imag_sf, k_filter[0], k_filter[1], mix_weight, normalizer
    )
    step_rows = math.gcd(share_rows * lax.axis_size("kvec"), 512)

    def one_block(counter, buffer):
        begin = counter * step_rows

        def compute(ignored):
            cosine, sine_part = phases(
                lax.dynamic_slice_in_dim(fractions, begin, step_rows, 1), wave_index
            )
            return jnp.dot(cosine, filt_real, precision=exact) - jnp.dot(
                sine_part, filt_imag, precision=exact
            )

        def nothing(ignored):
            return jnp.zeros((step_rows, feat_width), jnp.float32)

        part_rows = lax.cond(begin < brick_live, compute, nothing, 0)
        return lax.dynamic_update_slice_in_dim(buffer, part_rows, counter * step_rows, 0)

    messages = lax.psum_scatter(
        lax.fori_loop(
            0,
            share_rows * lax.axis_size("kvec") // step_rows,
            one_block,
            jnp.zeros((share_rows * lax.axis_size("kvec"), feat_width), jnp.float32),
        ),
        "kvec",
        scatter_dimension=0,
        tiled=True,
    )
    residual = features + jnp.dot(messages, out_weight, precision=exact)
    normed = (
        residual
        * lax.rsqrt(jnp.mean(residual * residual, axis=1, keepdims=True) + 1e-06)
        * norm_gain
    )
    hidden = jax.nn.silu(jnp.dot(normed, up_weight, precision=exact))
    return (residual + jnp.dot(hidden, down_weight, precision=exact)) * live_mask[:, None]


def solution(mesh):
    return jax.shard_map(
        shards,
        mesh=mesh,
        in_specs=(
            P(("atom", "kvec"), None),
            P(None, "atom"),
            P(None, "kvec"),
            P(),
            P(),
            P(None, "kvec", None),
            P(),
            P(),
            P(),
            P(),
            P(),
        ),
        out_specs=P(("atom", "kvec"), None),
        check_vma=False,
    )
```

profile of v0, /device:TPU:24, one launch (start us, length us, event | category | flops | bytes accessed | tf_op | source)
XLA Modules:
  0.0 225.0 jit_solution(8752469767851542707)
XLA Ops:
  6.5 0.0 all-gather.2.cloned.1.call-start
  6.6 1.3 fusion.60
  7.9 0.6 fusion.59
  8.5 2.3 %convolution_multiply_fusion = f32[384,256]{1,0:T(8,128)} fusion(f32[384,256]{1,0:T(8,128)} %param.17, f32[256,256]{1,0:T(8,128)} %param.21, f32[384]{0:T(512)S(1)} %fusion.59), kind=kOutput, calls=%fused_computation.48 | convolution fusion | flops 302088192 | bytes 1050112 | tf_op jit(solution)/shard_map/dot_general | solution.py:61
  10.8 0.0 all-gather.2.cloned.1.call-update
  10.8 0.0 all-reduce.3.cloned.1.call-start
  11.4 31.3 %all-gather.2.cloned.1.call-done = f32[1536,256]{1,0:T(8,128)} async-done(((f32[384,256]{1,0:T(8,128)}), f32[1536,256]{1,0:T(8,128)}) %all-gather.2.cloned.1.call-update) | async-done | bytes 1572880 | tf_op jit(solution)/shard_map/all_gather | solution.py:63
  42.8 0.0 copy-done.8
  42.9 0.0 copy-done.10
  42.9 28.3 %while.27 = (s32[]{:T(128)}, f32[512,256]{1,0:T(8,128)S(1)}, f32[512,256]{1,0:T(8,128)S(1)}, s32[]{:T(128)}, s32[3,1536]{1,0:T(4,128)S(1)}, /*index=5*/s32[3,512...) while((s32[]{:T(128)}, f32[512,256]{1,0:T(8,128)S(1)}, ...), condition=%wide.region_2.3_spmd, body=%wide.region_1.2_spmd.sunk | while | flops 1620312064 | bytes 3195095 | solution.py:82
  42.9 0.1 constant_dynamic-slice_fusion.3
  43.0 7.0 %convolution_subtract_fusion.4 = f32[512,256]{1,0:T(8,128)S(1)} fusion(f32[512,256]{1,0:T(8,128)S(1)} %get-tuple-element.414, s32[512]{0:T(512)S(1)} %bitcast.68, s32[512]{0:T(512)S(1)} %bitcast.64, s32[512]{0:T(512)S(1)} %bitcast.66, s32[512]{0:T(512)S(1)} %bitcast.62, s32[512]{0:T(512)S(1)} %bitcast.70, s32[512]{0:T(512)S(1)} %bitcast.60, ...), kind=kOutput, calls=%fused_computation.3.clone.1 | convolution fusion | flops 810156032 | bytes 1585156 | tf_op jit(solution)/shard_map/while/body/dot_general | solution.py:75
  50.0 6.9 %convolution_add_fusion.5 = f32[512,256]{1,0:T(8,128)S(1)} fusion(f32[512,256]{1,0:T(8,128)S(1)} %get-tuple-element.413, s32[512]{0:T(512)S(1)} %bitcast.69, s32[512]{0:T(512)S(1)} %bitcast.65, s32[512]{0:T(512)S(1)} %bitcast.67, s32[512]{0:T(512)S(1)} %bitcast.63, s32[512]{0:T(512)S(1)} %bitcast.71, s32[512]{0:T(512)S(1)} %bitcast.61, ...), kind=kOutput, calls=%fused_computation.4.clone.1 | convolution fusion | flops 810156032 | bytes 1585156 | tf_op jit(solution)/shard_map/while/body/dot_general | solution.py:72
  56.9 0.1 constant_dynamic-slice_fusion.3
  57.0 7.0 %convolution_subtract_fusion.4 = f32[512,256]{1,0:T(8,128)S(1)} fusion(f32[512,256]{1,0:T(8,128)S(1)} %get-tuple-element.414, s32[512]{0:T(512)S(1)} %bitcast.68, s32[512]{0:T(512)S(1)} %bitcast.64, s32[512]{0:T(512)S(1)} %bitcast.66, s32[512]{0:T(512)S(1)} %bitcast.62, s32[512]{0:T(512)S(1)} %bitcast.70, s32[512]{0:T(512)S(1)} %bitcast.60, ...), kind=kOutput, calls=%fused_computation.3.clone.1 | convolution fusion | flops 810156032 | bytes 1585156 | tf_op jit(solution)/shard_map/while/body/dot_general | solution.py:75
  64.0 6.9 %convolution_add_fusion.5 = f32[512,256]{1,0:T(8,128)S(1)} fusion(f32[512,256]{1,0:T(8,128)S(1)} %get-tuple-element.413, s32[512]{0:T(512)S(1)} %bitcast.69, s32[512]{0:T(512)S(1)} %bitcast.65, s32[512]{0:T(512)S(1)} %bitcast.67, s32[512]{0:T(512)S(1)} %bitcast.63, s32[512]{0:T(512)S(1)} %bitcast.71, s32[512]{0:T(512)S(1)} %bitcast.61, ...), kind=kOutput, calls=%fused_computation.4.clone.1 | convolution fusion | flops 810156032 | bytes 1585156 | tf_op jit(solution)/shard_map/while/body/dot_general | solution.py:72
  71.2 0.0 copy-start.6
  71.2 0.8 copy-done.3
  72.0 0.2 copy-done.4
  72.1 0.0 all-reduce.3.cloned.1.call-update
  72.2 0.0 reduce-scatter.2.cloned.1.call-start
  72.2 70.8 %all-reduce.3.cloned.1.call-done = (f32[512,256]{1,0:T(8,128)}, f32[512,256]{1,0:T(8,128)}) async-done(((f32[512,256]{1,0:T(8,128)}, f32[512,256]{1,0:T(8,128)}), (f32[512,256]{1,0:T(8,128)}, f32[512,256]{1,0:T(8,128)})) %all-reduce.3.cloned.1.call-update) | async-done | bytes 1048592 | tf_op jit(solution)/shard_map/psum | solution.py:83
  143.0 1.5 fusion.42
  144.5 0.6 fusion.47
  145.1 0.6 fusion.51
  145.7 0.6 fusion.34
  146.3 1.4 fusion.33
  147.7 0.1 broadcast_in_dim.6
  147.8 23.0 %while.28 = (s32[]{:T(128)}, f32[1536,256]{1,0:T(8,128)S(1)}, s32[]{:T(128)}, s32[3,1536]{1,0:T(4,128)S(1)}, s32[3,512]{1,0:T(4,128)S(1)}, /*index=5*/f32[512,25...) while((s32[]{:T(128)}, f32[1536,256]{1,0:T(8,128)S(1)}, ...), condition=%wide.region_8.9_spmd, body=%wide.region_5.8_spmd.sunk | while | flops 1620180992 | bytes 5816639 | solution.py:107
  148.6 10.3 %conditional.2 = (f32[512,256]{1,0:T(8,128)S(1)}) conditional(s32[]{:T(128)} %convert_element_type.48, () %tuple.75, (s32[]{:T(128)}, s32[3,1536]{1,0:T(4,128)S(1)}, s32[3,512]{1,0:T(4,128)S(1)}, f32[512,256]{1,0:T(8,128)S(1)}, f32[512,256]{1,0:T(8,128)}) %tuple.76), branch_computations={%region_6.6_spmd, %region_7.7_spmd} | conditional | flops 1620180992 | bytes 4767850 | solution.py:103
  148.6 0.1 constant_dynamic-slice_fusion.1
  148.7 5.0 %fusion.21 = f32[512,256]{1,0:T(8,128)S(1)} fusion(f32[512,256]{1,0:T(8,128)S(1)} %get-tuple-element.232, s32[512]{0:T(512)S(1)} %bitcast.80, s32[512]{0:T(512)S(1)} %bitcast.76, s32[512]{0:T(512)S(1)} %bitcast.78, s32[512]{0:T(512)S(1)} %bitcast.74, s32[512]{0:T(512)S(1)} %bitcast.82, s32[512]{0:T(512)S(1)} %bitcast.72), kind=kOutput, calls=%fused_computation.29 | convolution fusion | flops 810024960 | bytes 1060864 | tf_op jit(solution)/shard_map/while/body/eval_jaxpr/cond/branch_1_fun/dot_general | solution.py:96
  153.8 5.1 %convolution_subtract_fusion.1 = f32[512,256]{1,0:T(8,128)S(1)} fusion(f32[512,256]{1,0:T(8,128)S(1)} %fusion.21, f32[512,256]{1,0:T(8,128)S(1)} %copy-done.7, s32[512]{0:T(512)S(1)} %bitcast.81, s32[512]{0:T(512)S(1)} %bitcast.77, s32[512]{0:T(512)S(1)} %bitcast.79, s32[512]{0:T(512)S(1)} %bitcast.75, s32[512]{0:T(512)S(1)} %bitcast.83, s32[512]{0:T(512)S(1)} %bitcast.73), kind=kOutput, calls=%fused_computation.24 | convolution fusion | flops 810156032 | bytes 1585152 | tf_op jit(solution)/shard_map/while/body/eval_jaxpr/cond/branch_1_fun/dot_general | solution.py:96
  159.5 10.3 %conditional.2 = (f32[512,256]{1,0:T(8,128)S(1)}) conditional(s32[]{:T(128)} %convert_element_type.48, () %tuple.75, (s32[]{:T(128)}, s32[3,1536]{1,0:T(4,128)S(1)}, s32[3,512]{1,0:T(4,128)S(1)}, f32[512,256]{1,0:T(8,128)S(1)}, f32[512,256]{1,0:T(8,128)}) %tuple.76), branch_computations={%region_6.6_spmd, %region_7.7_spmd} | conditional | flops 1620180992 | bytes 4767850 | solution.py:103
  159.5 0.1 constant_dynamic-slice_fusion.1
  159.6 5.0 %fusion.21 = f32[512,256]{1,0:T(8,128)S(1)} fusion(f32[512,256]{1,0:T(8,128)S(1)} %get-tuple-element.232, s32[512]{0:T(512)S(1)} %bitcast.80, s32[512]{0:T(512)S(1)} %bitcast.76, s32[512]{0:T(512)S(1)} %bitcast.78, s32[512]{0:T(512)S(1)} %bitcast.74, s32[512]{0:T(512)S(1)} %bitcast.82, s32[512]{0:T(512)S(1)} %bitcast.72), kind=kOutput, calls=%fused_computation.29 | convolution fusion | flops 810024960 | bytes 1060864 | tf_op jit(solution)/shard_map/while/body/eval_jaxpr/cond/branch_1_fun/dot_general | solution.py:96
  164.7 5.1 %convolution_subtract_fusion.1 = f32[512,256]{1,0:T(8,128)S(1)} fusion(f32[512,256]{1,0:T(8,128)S(1)} %fusion.21, f32[512,256]{1,0:T(8,128)S(1)} %copy-done.7, s32[512]{0:T(512)S(1)} %bitcast.81, s32[512]{0:T(512)S(1)} %bitcast.77, s32[512]{0:T(512)S(1)} %bitcast.79, s32[512]{0:T(512)S(1)} %bitcast.75, s32[512]{0:T(512)S(1)} %bitcast.83, s32[512]{0:T(512)S(1)} %bitcast.73), kind=kOutput, calls=%fused_computation.24 | convolution fusion | flops 810156032 | bytes 1585152 | tf_op jit(solution)/shard_map/while/body/eval_jaxpr/cond/branch_1_fun/dot_general | solution.py:96
  170.4 0.1 conditional.2
  170.8 0.0 copy-start.5
  170.8 0.0 copy-start.9
  170.8 0.0 copy-start.11
  170.9 1.1 copy-done.1
  172.0 0.0 reduce-scatter.2.cloned.1.call-update
  172.0 0.0 copy-start.12
  172.0 42.3 %reduce-scatter.2.cloned.1.call-done = f32[384,256]{1,0:T(8,128)} async-done(((f32[1536,256]{1,0:T(8,128)}), f32[384,256]{1,0:T(8,128)}) %reduce-scatter.2.cloned.1.call-update) | async-done | bytes 393232 | tf_op jit(solution)/shard_map/reduce_scatter | solution.py:106
  214.3 1.6 multiply_reduce_fusion
  215.9 0.9 fusion.44
  216.8 1.7 fusion.35
  (25 shorter events, 0.3 us)
Async XLA Ops:
  6.5 209.4 %copy-start = (f32[256,512]{1,0:T(8,128)S(1)}, f32[256,512]{1,0:T(8,128)}, u32[]{:S(2)}) copy-start(f32[256,512]{1,0:T(8,128)} %param.26) | copy-start | bytes 1572868
  6.5 36.3 %copy-start.8 = (s32[3,512]{1,0:T(4,128)S(1)}, s32[3,512]{1,0:T(4,128)}, u32[]{:S(2)}) copy-start(s32[3,512]{1,0:T(4,128)} %param.19) | copy-start | bytes 18436
  6.5 36.3 %copy-start.10 = (s32[3,1536]{1,0:T(4,128)S(1)}, s32[3,1536]{1,0:T(4,128)}, u32[]{:S(2)}) copy-start(s32[3,1536]{1,0:T(4,128)} %param.18) | copy-start | bytes 55300
  6.5 36.2 %all-gather.2.cloned.1.call-start = ((), (), s32[]{:S(2)}) async-start(), calls=%async_computation.1 | async-start | bytes 1966080 | tf_op jit(solution)/shard_map/all_gather | solution.py:63
  10.8 132.2 %all-reduce.3.cloned.1.call-start = ((), (), s32[]{:S(2)}) async-start(), calls=%async_computation.3 | async-start | bytes 2097152 | tf_op jit(solution)/shard_map/psum | solution.py:83
  71.2 0.8 copy-start.3
  71.2 1.0 copy-start.4
  71.2 71.9 %copy-start.6 = (f32[2,512,256]{2,1,0:T(8,128)S(1)}, f32[2,512,256]{2,1,0:T(8,128)}, u32[]{:S(2)}) copy-start(f32[2,512,256]{2,1,0:T(8,128)} %param.22) | copy-start | bytes 3145732
  72.2 142.2 %reduce-scatter.2.cloned.1.call-start = ((), (), s32[]{:S(2)}) async-start(), calls=%async_computation.2 | async-start | bytes 1966080 | tf_op jit(solution)/shard_map/reduce_scatter | solution.py:106
  143.0 1.5 copy-start.2
  148.7 5.1 %copy-start.7 = (f32[512,256]{1,0:T(8,128)S(1)}, f32[512,256]{1,0:T(8,128)}, u32[]{:S(2)}) copy-start(f32[512,256]{1,0:T(8,128)} %get-tuple-element.233) | copy-start | bytes 1572868 | tf_op jit(solution)/shard_map/while/body/eval_jaxpr/cond
  159.6 5.0 %copy-start.7 = (f32[512,256]{1,0:T(8,128)S(1)}, f32[512,256]{1,0:T(8,128)}, u32[]{:S(2)}) copy-start(f32[512,256]{1,0:T(8,128)} %get-tuple-element.233) | copy-start | bytes 1572868 | tf_op jit(solution)/shard_map/while/body/eval_jaxpr/cond
  170.8 1.2 copy-start.1
  170.8 43.5 %copy-start.5 = (f32[384,256]{1,0:T(8,128)S(1)}, f32[384,256]{1,0:T(8,128)}, u32[]{:S(2)}) copy-start(f32[384,256]{1,0:T(8,128)} %param.17) | copy-start | bytes 1179652
  170.8 43.5 %copy-start.9 = (f32[256,256]{1,0:T(8,128)S(1)}, f32[256,256]{1,0:T(8,128)}, u32[]{:S(2)}) copy-start(f32[256,256]{1,0:T(8,128)} %param.24) | copy-start | bytes 786436
  170.8 45.1 %copy-start.11 = (f32[256]{0:T(256)S(1)}, f32[256]{0:T(256)}, u32[]{:S(2)}) copy-start(f32[256]{0:T(256)} %param.25) | copy-start | bytes 3076
  172.0 44.8 %copy-start.12 = (f32[512,256]{1,0:T(8,128)S(1)}, f32[512,256]{1,0:T(8,128)}, u32[]{:S(2)}) copy-start(f32[512,256]{1,0:T(8,128)} %param.27) | copy-start | bytes 1572868
Sparse Core Ops, SparseCore 0:
  10.9 31.8 all-gather.1
  72.3 70.6 all-reduce.2
  172.1 42.1 reduce-scatter.1
where the time goes:
time: 226 us; the launch traced here: 225 us
  waiting for transfers between devices  145 us (64%)
  matrix products  57.7 us (26%)
  between operations  13.9 us (6%)
  other arithmetic  3.37 us (1%)
  local copies, waits for them, and re-layouts  2.81 us (1%)
  loops' own time  2.65 us (1%)
    psum x1, waiting for transfers between devices, shards(): real_sf, imag_sf = lax.psum((real_sf, imag_sf), 'atom')  70.8 us
    reduce_scatter x1, waiting for transfers between devices, shards(): lax.psum_scatter(lax.fori_loop(0, share_rows * lax.axis_size('kvec') // s...  42.3 us
    all_gather x1, waiting for transfers between devices, shards(): values = lax.all_gather(projected, 'kvec', axis=0, tiled=True)  31.3 us
    dot_general x2, matrix products, accumulate(): lax.dot_general(sine_part, value_rows, contract, precision=exact)  14 us
    dot_general x2, matrix products, accumulate(): lax.dot_general(cosine, value_rows, contract, precision=exact)  13.9 us
    dot_general x2, matrix products, compute(): jnp.dot(sine_part, filt_imag, precision=exact)  10.2 us
    dot_general x2, matrix products, compute(): jnp.dot(cosine, filt_real, precision=exact)  10.1 us
  transfers between devices with their start and end apart: 3, of which 3 were waited for; matrix products, arithmetic and copies ran while one was open for 0% of the time, Pallas kernels for 0%

commit v1 on v0

v1 whole, which is shorter than its diff:
```python
import functools
import math

import jax
import jax.numpy as jnp
from jax import lax
from jax.experimental import pallas as pl
from jax.experimental.pallas import tpu as pltpu
from jax.sharding import PartitionSpec as P

SIN_POLY = (3.141592640130707, -5.167710083507862, 2.550077523214134, -0.5982912856178576, 0.0776576603009221)
COS_POLY = (0.9999999997799045, -4.9348021370788056, 4.058709159555753, -1.3352120030448535, 0.23493731379172217, -0.024396324310603436)
MESH = pl.DeviceIdType.MESH
f32 = jnp.float32
bf16 = jnp.bfloat16


def horner(coefs, y):
    acc = jnp.full_like(y, coefs[-1])
    for c in coefs[-2::-1]:
        acc = acc * y + c
    return acc


def split(x):
    hi = x.astype(bf16)
    return hi, (x - hi.astype(f32)).astype(bf16)


def mm(a, b):
    return jnp.dot(a, b, preferred_element_type=f32)


def mm3(a, b):
    return mm(a[0], b[0]) + (mm(a[0], b[1]) + mm(a[1], b[0]))


def kernel(
    groups,
    bricks,
    normalizer,
    count_ref,
    feat_ref,
    frac_t_ref,
    frac_n_ref,
    wave_t_ref,
    wave_n_ref,
    gain_ref,
    kf_hbm,
    vw_hbm,
    mix_hbm,
    ow_hbm,
    up_hbm,
    down_hbm,
    out_ref,
    kf,
    vw,
    mix,
    ow,
    up,
    down,
    phase_t,
    phase_n,
    ct,
    cn,
    xbuf,
    sacc,
    pbuf,
    ssum,
    rbuf,
    tsl,
    tbuf,
    mbuf,
    gbuf,
    load_sem,
    x_send,
    x_recv,
    p_send,
    p_recv,
    r_send,
    r_recv,
    t_send,
    t_recv,
    q_send,
    q_recv,
    m_send,
    m_recv,
):
    rows, width = feat_ref.shape
    k_shard = kf.shape[1]
    half = k_shard // 2
    z_size = bricks // 2
    piece = half // z_size
    a = lax.axis_index("atom")
    g = lax.axis_index("kvec")
    z = lax.div(a, 2)
    c = lax.rem(a, 2)
    partner = 2 * z + 1 - c
    count = count_ref[0]

    def z_peer(d):
        return 2 * lax.rem(z + d, z_size) + c

    def z_from(d):
        return lax.rem(z + z_size - d, z_size)

    barrier = pltpu.get_barrier_semaphore()
    for d in range(1, groups):
        pl.semaphore_signal(
            barrier, inc=1, device_id={"kvec": lax.rem(g + d, groups)}, device_id_type=MESH
        )
    for d in range(1, z_size):
        pl.semaphore_signal(
            barrier, inc=1, device_id={"atom": z_peer(d)}, device_id_type=MESH
        )
    pl.semaphore_signal(barrier, inc=1, device_id={"atom": partner}, device_id_type=MESH)

    loads = []
    for i, (src, dst) in enumerate(
        ((kf_hbm, kf), (vw_hbm, vw), (mix_hbm, mix), (ow_hbm, ow), (up_hbm, up), (down_hbm, down))
    ):
        loads.append(pltpu.make_async_copy(src, dst, load_sem.at[i]))
        loads[-1].start()

    pl.semaphore_wait(barrier, groups - 1 + z_size)

    def x_copy(d):
        return pltpu.make_async_remote_copy(
            src_ref=feat_ref,
            dst_ref=xbuf.at[g],
            send_sem=x_send.at[d - 1],
            recv_sem=x_recv.at[d - 1],
            device_id={"kvec": lax.rem(g + d, groups)},
            device_id_type=MESH,
        )

    for d in range(1, groups):
        x_copy(d).start()

    def table(dst, j, phase, lead, step):
        def one(i, carry):
            at = pl.multiple_of(i * step, step)
            x = phase[pl.ds(at, step), :]
            r = x - jnp.floor(x + 0.5)
            y = r * r
            s = r * horner(SIN_POLY, y)
            co = horner(COS_POLY, y)
            s2 = s + s
            chi, clo = split(1.0 - s2 * s)
            shi, slo = split(s2 * co)
            dst[0, j, pl.ds(at, step), :] = chi
            dst[1, j, pl.ds(at, step), :] = clo
            dst[2, j, pl.ds(at, step), :] = shi
            dst[3, j, pl.ds(at, step), :] = slo
            return carry

        lax.fori_loop(0, lead // step, one, 0, unroll=2)

    def make_tables(j, carry):
        phase_t[...] = mm(wave_t_ref[...], frac_t_ref[j])
        table(ct, j, phase_t, k_shard, 32)
        phase_n[...] = mm(frac_n_ref[j], wave_n_ref[...])
        table(cn, j, phase_n, rows, 16)
        return carry

    lax.fori_loop(0, groups, make_tables, 0)

    def live(j):
        spot = lax.broadcasted_iota(jnp.int32, (rows, width), 0) + j * rows
        return spot < count

    def gather_term(x, j):
        v = split(jnp.where(live(j), x, 0.0))
        re = mm3((ct[0, j], ct[1, j]), v)
        im = mm3((ct[2, j], ct[3, j]), v)
        return (
            re.reshape(2, z_size, piece, width),
            im.reshape(2, z_size, piece, width),
        )

    re, im = gather_term(feat_ref[...], g)
    sacc[:, :, 0] = re
    sacc[:, :, 1] = im

    def take_block(d, carry):
        j = lax.rem(g + groups - d, groups)
        x_copy(d).wait_recv()
        re, im = gather_term(xbuf[j], j)
        sacc[:, :, 0] += re
        sacc[:, :, 1] += im
        return carry

    lax.fori_loop(1, groups, take_block, 0)

    pair = pltpu.make_async_remote_copy(
        src_ref=sacc.at[1 - c],
        dst_ref=pbuf,
        send_sem=p_send,
        recv_sem=p_recv,
        device_id={"atom": partner},
        device_id_type=MESH,
    )
    pair.start()
    pair.wait_recv()
    ssum[...] = sacc[c] + pbuf[...]

    def r_copy(d):
        return pltpu.make_async_remote_copy(
            src_ref=ssum.at[lax.rem(z + d, z_size)],
            dst_ref=rbuf.at[d - 1],
            send_sem=r_send.at[d - 1],
            recv_sem=r_recv.at[d - 1],
            device_id={"atom": z_peer(d)},
            device_id_type=MESH,
        )

    for d in range(1, z_size):
        r_copy(d).start()
    for load in loads:
        load.wait()
    vws = split(vw[...])
    mix_re = split(mix[0])
    mix_im = split(mix[1])
    total = ssum[z]
    for d in range(1, z_size):
        r_copy(d).wait_recv()
        total = total + rbuf[d - 1]
    sv = mm3(split(total.reshape(2 * piece, width)), vws)
    sre = sv[:piece]
    sim = -sv[piece:]
    at = pl.multiple_of(c * half + z * piece, piece)
    k_re = kf[0, pl.ds(at, piece), :]
    k_im = kf[1, pl.ds(at, piece), :]
    u_re = split(sre * k_re - sim * k_im)
    u_im = split(sre * k_im + sim * k_re)
    tsl[0] = (mm3(u_re, mix_re) - mm3(u_im, mix_im)) * normalizer
    tsl[1] = (mm3(u_re, mix_im) + mm3(u_im, mix_re)) * normalizer

    def t_copy(d):
        return pltpu.make_async_remote_copy(
            src_ref=tsl,
            dst_ref=tbuf.at[c, z],
            send_sem=t_send.at[d - 1],
            recv_sem=t_recv.at[d - 1],
            device_id={"atom": z_peer(d)},
            device_id_type=MESH,
        )

    def q_copy(d):
        return pltpu.make_async_remote_copy(
            src_ref=tsl if d == 0 else tbuf.at[c, z_from(d)],
            dst_ref=tbuf.at[c, z_from(d)],
            send_sem=q_send.at[d],
            recv_sem=q_recv.at[d],
            device_id={"atom": partner},
            device_id_type=MESH,
        )

    for d in range(1, z_size):
        t_copy(d).start()
    q_copy(0).start()
    tbuf[c, z] = tsl[...]
    for d in range(1, z_size):
        t_copy(d).wait_recv()
        q_copy(d).start()
    for d in range(z_size):
        q_copy(d).wait_recv()

    t_re = split(tbuf[:, :, 0].reshape(k_shard, width))
    t_im = split(tbuf[:, :, 1].reshape(k_shard, width))

    def message(j):
        return mm3((cn[0, j], cn[1, j]), t_re) - mm3((cn[2, j], cn[3, j]), t_im)

    def m_copy(d):
        return pltpu.make_async_remote_copy(
            src_ref=mbuf.at[d - 1],
            dst_ref=gbuf.at[d - 1],
            send_sem=m_send.at[d - 1],
            recv_sem=m_recv.at[d - 1],
            device_id={"kvec": lax.rem(g + d, groups)},
            device_id_type=MESH,
        )

    def give_block(d, carry):
        mbuf[d - 1] = message(lax.rem(g + d, groups))
        m_copy(d).start()
        return carry

    lax.fori_loop(1, groups, give_block, 0)
    own = message(g)
    for d in range(1, groups):
        m_copy(d).wait_recv()
        own = own + gbuf[d - 1]

    residual = feat_ref[...] + mm3(split(own), split(ow[...]))
    scale = lax.rsqrt(jnp.mean(residual * residual, axis=1, keepdims=True) + 1e-06)
    normed = residual * scale * gain_ref[...]
    raised = mm3(split(normed), split(up[...]))
    hidden = raised / (1.0 + jnp.exp(-raised))
    result = residual + mm3(split(hidden), split(down[...]))
    out_ref[...] = jnp.where(live(g), result, 0.0)

    for d in range(1, groups):
        x_copy(d).wait_send()
        m_copy(d).wait_send()
    pair.wait_send()
    for d in range(1, z_size):
        r_copy(d).wait_send()
        t_copy(d).wait_send()
    for d in range(z_size):
        q_copy(d).wait_send()


def shards(
    features,
    fractions,
    wave_index,
    brick_count,
    value_weight,
    k_filter,
    mix_weight,
    out_weight,
    norm_gain,
    up_weight,
    down_weight,
):
    rows, width = features.shape
    groups = lax.axis_size("kvec")
    bricks = lax.axis_size("atom")
    k_shard = wave_index.shape[1]
    hidden = up_weight.shape[1]
    capacity = rows * groups
    z_size = bricks // 2
    piece = k_shard // bricks
    normalizer = 1.0 / math.sqrt(bricks * capacity // 2 * (k_shard * groups))
    own_brick = lax.axis_index("atom")
    brick_ids = jnp.arange(bricks, dtype=jnp.int32)
    count = jnp.sum(jnp.where(brick_ids == own_brick, brick_count, 0)).reshape(1)

    frac = jnp.concatenate(
        [
            (fractions >> 5).astype(f32) * (1.0 / 32),
            (fractions & 31).astype(f32) * (1.0 / 1024),
            jnp.zeros((10, capacity), f32),
        ],
        axis=0,
    ).astype(bf16)
    frac_t = frac.reshape(16, groups, rows).transpose(1, 0, 2)
    frac_n = frac.reshape(16, groups, rows).transpose(1, 2, 0)
    wave = wave_index.astype(f32)
    wave_n = jnp.concatenate([wave, wave, jnp.zeros((10, k_shard), f32)], axis=0).astype(bf16)
    wave_t = wave_n.T

    vmem = pl.BlockSpec(memory_space=pltpu.VMEM)
    hbm = pl.BlockSpec(memory_space=pl.ANY)
    dma = pltpu.SemaphoreType.DMA
    return pl.pallas_call(
        functools.partial(kernel, groups, bricks, normalizer),
        out_shape=jax.ShapeDtypeStruct((rows, width), f32),
        in_specs=[pl.BlockSpec(memory_space=pltpu.SMEM)] + [vmem] * 6 + [hbm] * 6,
        out_specs=vmem,
        scratch_shapes=[
            pltpu.VMEM((2, k_shard, width), f32),
            pltpu.VMEM((width, width), f32),
            pltpu.VMEM((2, width, width), f32),
            pltpu.VMEM((width, width), f32),
            pltpu.VMEM((width, hidden), f32),
            pltpu.VMEM((hidden, width), f32),
            pltpu.VMEM((k_shard, rows), f32),
            pltpu.VMEM((rows, k_shard), f32),
            pltpu.VMEM((4, groups, k_shard, rows), bf16),
            pltpu.VMEM((4, groups, rows, k_shard), bf16),
            pltpu.VMEM((groups, rows, width), f32),
            pltpu.VMEM((2, z_size, 2, piece, width), f32),
            pltpu.VMEM((z_size, 2, piece, width), f32),
            pltpu.VMEM((z_size, 2, piece, width), f32),
            pltpu.VMEM((z_size - 1, 2, piece, width), f32),
            pltpu.VMEM((2, piece, width), f32),
            pltpu.VMEM((2, z_size, 2, piece, width), f32),
            pltpu.VMEM((groups - 1, rows, width), f32),
            pltpu.VMEM((groups - 1, rows, width), f32),
            dma((6,)),
            dma((groups - 1,)),
            dma((groups - 1,)),
            dma,
            dma,
            dma((z_size - 1,)),
            dma((z_size - 1,)),
            dma((z_size - 1,)),
            dma((z_size - 1,)),
            dma((z_size,)),
            dma((z_size,)),
            dma((groups - 1,)),
            dma((groups - 1,)),
        ],
        compiler_params=pltpu.CompilerParams(
            collective_id=0, has_side_effects=True, vmem_limit_bytes=56 * 1024 * 1024
        ),
    )(
        count,
        features,
        frac_t,
        frac_n,
        wave_t,
        wave_n,
        norm_gain.reshape(1, width),
        k_filter,
        value_weight,
        mix_weight,
        out_weight,
        up_weight,
        down_weight,
    )


def solution(mesh):
    return jax.shard_map(
        shards,
        mesh=mesh,
        in_specs=(
            P(("atom", "kvec"), None),
            P(None, "atom"),
            P(None, "kvec"),
            P(),
            P(),
            P(None, "kvec", None),
            P(),
            P(),
            P(),
            P(),
            P(),
        ),
        out_specs=P(("atom", "kvec"), None),
        check_vma=False,
    )
```

time: 226 us -> 84.7 us (0.37)
  waiting for transfers between devices: 145 us -> 0 us
  Pallas kernels: 0 us -> 76.3 us
  matrix products: 57.7 us -> 0 us
  between operations: 13.9 us -> 0.02 us
  loops' own time: 2.65 us -> 0 us
    pallas_call x0 -> x1, Pallas kernels: none -> 76.3 us  [shards(): pl.pallas_call(functools.partial(kernel, groups, bricks, normalizer), out...]
    psum x1 -> x0, waiting for transfers between devices: 70.8 us -> none  [shards(): real_sf, imag_sf = lax.psum((real_sf, imag_sf), 'atom')]
    dot_general x16 -> x0, matrix products: 57.7 us -> none  [the longest x2 14 us: accumulate(): lax.dot_general(sine_part, value_rows, contract, precision=exact)]
    reduce_scatter x1 -> x0, waiting for transfers between devices: 42.3 us -> none  [shards(): lax.psum_scatter(lax.fori_loop(0, share_rows * lax.axis_size('kvec') // s...]
    all_gather x1 -> x0, waiting for transfers between devices: 31.3 us -> none  [shards(): values = lax.all_gather(projected, 'kvec', axis=0, tiled=True)]
    another operation x5 -> x0, loops' own time: 2.65 us -> none  [the longest x1 2.29 us: shards(): lax.fori_loop(0, share_rows * lax.axis_size('kvec') // step_rows, one_blo...]
  transfers between devices with their start and end apart: 3 -> 0, of which waited for: 3 -> 0; matrix products, arithmetic and copies ran while one was open for 0% -> 0% of each run, Pallas kernels for 0% -> 0%
where the time goes in v1:
time: 84.7 us; the launch traced here: 83.3 us
  Pallas kernels  76.3 us (90%)
  local copies, waits for them, and re-layouts  3.52 us (4%)
  other arithmetic  3.46 us (4%)
    pallas_call x1, Pallas kernels, shards(): pl.pallas_call(functools.partial(kernel, groups, bricks, normalizer), out...  76.3 us
    unnamed x3, local copies, waits for them, and re-layouts  1.77 us

profile of v1, /device:TPU:24, one launch (start us, length us, event | category | flops | bytes accessed | tf_op | source)
XLA Modules:
  0.0 83.3 jit_solution(1212498656011752463)
XLA Ops:
  0.0 0.0 copy-start
  0.0 1.4 %fusion = s32[]{:T(128)} fusion(s32[8]{0:T(128)} %param.14, s32[]{:T(128)S(6)} %axis_index.15), kind=kLoop, calls=%fused_computation.6 | loop fusion | flops 23 | bytes 40 | tf_op jit(solution)/shard_map/reduce_sum | solution.py:339
  1.4 0.1 pad.5.clone
  1.5 0.7 convert_convert_fusion
  2.2 0.0 copy-done
  2.2 0.7 maximum_maximum_fusion.1
  2.9 0.7 maximum_maximum_fusion
  3.6 0.7 copy.17.wave_t_ref
  4.3 0.9 %copy.16 = bf16[16,4,384]{0,2,1:T(8,128)(2,1)} copy(bf16[16,4,384]{2,0,1:T(8,128)(2,1)S(1)} %get-tuple-element.5) | data formatting | bytes 98304 | tf_op jit(solution)/shard_map/concatenate | solution.py:341
  5.2 76.3 %shard_map.109 = f32[384,256]{1,0:T(8,128)} custom-call(s32[1]{0:T(128)} %bitcast.count_ref, f32[384,256]{1,0:T(8,128)} %feat_ref.1, bf16[4,16,384]{2,1,0:T(8,128)(2,1)} %get-tuple-element.6.frac_t_ref, bf16[4,384,16]{2,1,0:T(8,128)(2,1)} %bitcast.9, bf16[512,16]{1,0:T(8,128)(2,1)} %copy.17.wave_t_ref, bf16[16,512]{1,0:T(8,128)(2,1)} %get-tuple-element.9.wave_n_ref, ...), custom_call_target="tpu_custom_call" | custom-call | tf_op jit(solution)/shard_map/pallas_call | solution.py:358
  81.6 1.8 %copy.19 = f32[384,256]{1,0:T(8,128)} copy(f32[384,256]{1,0:T(8,128)} %shard_map.109) | data formatting | bytes 786432
  (2 shorter events, 0.0 us)
Async XLA Ops:
  0.0 2.2 %copy-start = (s32[3,1536]{1,0:T(4,128)S(1)}, s32[3,1536]{1,0:T(4,128)}, u32[]{:S(2)}) copy-start(s32[3,1536]{1,0:T(4,128)} %param.12) | copy-start | bytes 55300

commit v2 on v1

v2 whole, which is shorter than its diff:
```python
import functools
import math

import jax
import jax.numpy as jnp
from jax import lax
from jax.experimental import pallas as pl
from jax.experimental.pallas import tpu as pltpu
from jax.sharding import PartitionSpec as P

SIN_POLY = (3.141592640130707, -5.167710083507862, 2.550077523214134, -0.5982912856178576, 0.0776576603009221)
COS_POLY = (0.9999999997799045, -4.9348021370788056, 4.058709159555753, -1.3352120030448535, 0.23493731379172217, -0.024396324310603436)
PARTS = 2
MESH = pl.DeviceIdType.MESH
f32 = jnp.float32
bf16 = jnp.bfloat16


def horner(coefs, y):
    acc = jnp.full_like(y, coefs[-1])
    for c in coefs[-2::-1]:
        acc = acc * y + c
    return acc


def split(x):
    hi = x.astype(bf16)
    return hi, (x - hi.astype(f32)).astype(bf16)


def mm(a, b):
    return jnp.dot(a, b, preferred_element_type=f32)


def mm3(a, b):
    return mm(a[0], b[0]) + (mm(a[0], b[1]) + mm(a[1], b[0]))


def kernel(
    groups,
    bricks,
    normalizer,
    count_ref,
    feat_ref,
    frac_ref,
    wave_ref,
    gain_ref,
    kf_hbm,
    vw_hbm,
    mix_hbm,
    ow_hbm,
    up_hbm,
    down_hbm,
    out_ref,
    kf,
    vw,
    mix,
    ow,
    up,
    down,
    frac,
    phase_t,
    phase_n,
    ct,
    cn,
    xbuf,
    sacc,
    pbuf,
    ssum,
    rbuf,
    tsl,
    tbuf,
    mbuf,
    gbuf,
    load_sem,
    x_send,
    x_recv,
    p_send,
    p_recv,
    r_send,
    r_recv,
    t_send,
    t_recv,
    q_send,
    q_recv,
    m_send,
    m_recv,
):
    rows, width = feat_ref.shape
    k_shard = kf.shape[1]
    half = k_shard // 2
    z_size = bricks // 2
    piece = half // z_size
    lanes = width // PARTS
    a = lax.axis_index("atom")
    g = lax.axis_index("kvec")
    z = lax.div(a, 2)
    c = lax.rem(a, 2)
    partner = 2 * z + 1 - c
    count = count_ref[a]

    def z_peer(d):
        return 2 * lax.rem(z + d, z_size) + c

    def z_from(d):
        return lax.rem(z + z_size - d, z_size)

    barrier = pltpu.get_barrier_semaphore()
    for d in range(1, groups):
        pl.semaphore_signal(
            barrier, inc=1, device_id={"kvec": lax.rem(g + d, groups)}, device_id_type=MESH
        )
    for d in range(1, z_size):
        pl.semaphore_signal(
            barrier, inc=1, device_id={"atom": z_peer(d)}, device_id_type=MESH
        )
    pl.semaphore_signal(barrier, inc=1, device_id={"atom": partner}, device_id_type=MESH)

    loads = []
    for i, (src, dst) in enumerate(
        ((kf_hbm, kf), (vw_hbm, vw), (mix_hbm, mix), (ow_hbm, ow), (up_hbm, up), (down_hbm, down))
    ):
        loads.append(pltpu.make_async_copy(src, dst, load_sem.at[i]))
        loads[-1].start()

    pl.semaphore_wait(barrier, groups - 1 + z_size)

    def x_copy(h, d):
        return pltpu.make_async_remote_copy(
            src_ref=feat_ref.at[:, h * lanes : (h + 1) * lanes],
            dst_ref=xbuf.at[h, g],
            send_sem=x_send.at[h, d - 1],
            recv_sem=x_recv.at[h, d - 1],
            device_id={"kvec": lax.rem(g + d, groups)},
            device_id_type=MESH,
        )

    for h in range(PARTS):
        for d in range(1, groups):
            x_copy(h, d).start()

    def table(dst, j, phase, lead, step):
        def one(i, carry):
            at = pl.multiple_of(i * step, step)
            x = phase[pl.ds(at, step), :]
            r = x - jnp.floor(x + 0.5)
            y = r * r
            s = r * horner(SIN_POLY, y)
            co = horner(COS_POLY, y)
            s2 = s + s
            chi, clo = split(1.0 - s2 * s)
            shi, slo = split(s2 * co)
            dst[0, j, pl.ds(at, step), :] = chi
            dst[1, j, pl.ds(at, step), :] = clo
            dst[2, j, pl.ds(at, step), :] = shi
            dst[3, j, pl.ds(at, step), :] = slo
            return carry

        lax.fori_loop(0, lead // step, one, 0, unroll=2)

    parts = frac_ref[...]
    stacked = jnp.concatenate(
        [
            (parts >> 5).astype(f32) * (1.0 / 32),
            (parts & 31).astype(f32) * (1.0 / 1024),
            jnp.zeros((2, groups * rows), f32),
        ],
        axis=0,
    )
    for j in range(groups):
        frac[j] = stacked[:, j * rows : (j + 1) * rows].astype(bf16)
    wave = wave_ref[...].astype(f32)
    wave = jnp.concatenate([wave, wave, jnp.zeros((2, k_shard), f32)], axis=0).astype(bf16)
    first = (((0,), (0,)), ((), ()))

    def make_tables(j, carry):
        phase_t[...] = lax.dot_general(wave, frac[j], first, preferred_element_type=f32)
        table(ct, j, phase_t, k_shard, 32)
        return carry

    def more_tables(j, carry):
        phase_n[...] = lax.dot_general(frac[j], wave, first, preferred_element_type=f32)
        table(cn, j, phase_n, rows, 16)
        return carry

    lax.fori_loop(0, groups, make_tables, 0)

    def live(j, cols):
        spot = lax.broadcasted_iota(jnp.int32, (rows, cols), 0) + j * rows
        return spot < count

    def twice(hi, lo, pair):
        both = mm(hi, pair)
        return both[:, :lanes] + (both[:, lanes:] + mm(lo, pair[:, :lanes]))

    def gather_term(x, j):
        v = jnp.concatenate(split(jnp.where(live(j, lanes), x, 0.0)), axis=1)
        re = twice(ct[0, j], ct[1, j], v)
        im = twice(ct[2, j], ct[3, j], v)
        return (
            re.reshape(2, z_size, piece, lanes),
            im.reshape(2, z_size, piece, lanes),
        )

    def own_block(h):
        re, im = gather_term(feat_ref[:, h * lanes : (h + 1) * lanes], g)
        sacc[h, :, :, 0] = re
        sacc[h, :, :, 1] = im

    def other_blocks(h):
        def take_block(d, carry):
            j = lax.rem(g + groups - d, groups)
            x_copy(h, d).wait_recv()
            re, im = gather_term(xbuf[h, j], j)
            sacc[h, :, :, 0] += re
            sacc[h, :, :, 1] += im
            return carry

        lax.fori_loop(1, groups, take_block, 0)

    def pair(h):
        return pltpu.make_async_remote_copy(
            src_ref=sacc.at[h, 1 - c],
            dst_ref=pbuf.at[h],
            send_sem=p_send.at[h],
            recv_sem=p_recv.at[h],
            device_id={"atom": partner},
            device_id_type=MESH,
        )

    def r_copy(h, d):
        return pltpu.make_async_remote_copy(
            src_ref=ssum.at[h, lax.rem(z + d, z_size)],
            dst_ref=rbuf.at[h, d - 1],
            send_sem=r_send.at[h, d - 1],
            recv_sem=r_recv.at[h, d - 1],
            device_id={"atom": z_peer(d)},
            device_id_type=MESH,
        )

    own_block(0)
    for h in range(PARTS):
        other_blocks(h)
        pair(h).start()
        if h + 1 < PARTS:
            own_block(h + 1)
        pair(h).wait_recv()
        ssum[h] = sacc[h, c] + pbuf[h]
        for d in range(1, z_size):
            r_copy(h, d).start()

    lax.fori_loop(0, groups, more_tables, 0)
    for load in loads:
        load.wait()
    vws = split(vw[...])
    mix_re = split(mix[0])
    mix_im = split(mix[1])
    totals = []
    for h in range(PARTS):
        total = ssum[h, z]
        for d in range(1, z_size):
            r_copy(h, d).wait_recv()
            total = total + rbuf[h, d - 1]
        totals.append(total.reshape(2 * piece, lanes))
    sv = mm3(split(jnp.concatenate(totals, axis=1)), vws)
    sre = sv[:piece]
    sim = -sv[piece:]
    at = pl.multiple_of(c * half + z * piece, piece)
    k_re = kf[0, pl.ds(at, piece), :]
    k_im = kf[1, pl.ds(at, piece), :]
    u_re = split(sre * k_re - sim * k_im)
    u_im = split(sre * k_im + sim * k_re)

    def t_copy(h, d):
        return pltpu.make_async_remote_copy(
            src_ref=tsl.at[h],
            dst_ref=tbuf.at[h, c, z],
            send_sem=t_send.at[h, d - 1],
            recv_sem=t_recv.at[h, d - 1],
            device_id={"atom": z_peer(d)},
            device_id_type=MESH,
        )

    def q_copy(h, d):
        return pltpu.make_async_remote_copy(
            src_ref=tsl.at[h] if d == 0 else tbuf.at[h, c, z_from(d)],
            dst_ref=tbuf.at[h, c, z_from(d)],
            send_sem=q_send.at[h, d],
            recv_sem=q_recv.at[h, d],
            device_id={"atom": partner},
            device_id_type=MESH,
        )

    def m_copy(h, d):
        return pltpu.make_async_remote_copy(
            src_ref=mbuf.at[h, d - 1],
            dst_ref=gbuf.at[h, d - 1],
            send_sem=m_send.at[h, d - 1],
            recv_sem=m_recv.at[h, d - 1],
            device_id={"kvec": lax.rem(g + d, groups)},
            device_id_type=MESH,
        )

    out_re = (mm3(u_re, mix_re) - mm3(u_im, mix_im)) * normalizer
    out_im = (mm3(u_re, mix_im) + mm3(u_im, mix_re)) * normalizer
    for h in range(PARTS):
        tsl[h, 0] = out_re[:, h * lanes : (h + 1) * lanes]
        tsl[h, 1] = out_im[:, h * lanes : (h + 1) * lanes]
        for d in range(1, z_size):
            t_copy(h, d).start()
        q_copy(h, 0).start()
        tbuf[h, c, z] = tsl[h]

    owns = []
    for h in range(PARTS):
        for d in range(1, z_size):
            t_copy(h, d).wait_recv()
            q_copy(h, d).start()
        for d in range(z_size):
            q_copy(h, d).wait_recv()
        t_re = jnp.concatenate(split(tbuf[h, :, :, 0].reshape(k_shard, lanes)), axis=1)
        t_im = jnp.concatenate(split(tbuf[h, :, :, 1].reshape(k_shard, lanes)), axis=1)

        def message(j):
            return twice(cn[0, j], cn[1, j], t_re) - twice(cn[2, j], cn[3, j], t_im)

        def give_block(d, carry):
            mbuf[h, d - 1] = message(lax.rem(g + d, groups))
            m_copy(h, d).start()
            return carry

        lax.fori_loop(1, groups, give_block, 0)
        owns.append(message(g))
    for h in range(PARTS):
        for d in range(1, groups):
            m_copy(h, d).wait_recv()
            owns[h] = owns[h] + gbuf[h, d - 1]
    own = jnp.concatenate(owns, axis=1)

    residual = feat_ref[...] + mm3(split(own), split(ow[...]))
    scale = lax.rsqrt(jnp.mean(residual * residual, axis=1, keepdims=True) + 1e-06)
    normed = residual * scale * gain_ref[...]
    raised = mm3(split(normed), split(up[...]))
    hidden = raised / (1.0 + jnp.exp(-raised))
    result = residual + mm3(split(hidden), split(down[...]))
    out_ref[...] = jnp.where(live(g, width), result, 0.0)

    for h in range(PARTS):
        pair(h).wait_send()
        for d in range(1, groups):
            x_copy(h, d).wait_send()
            m_copy(h, d).wait_send()
        for d in range(1, z_size):
            r_copy(h, d).wait_send()
            t_copy(h, d).wait_send()
        for d in range(z_size):
            q_copy(h, d).wait_send()


def shards(
    features,
    fractions,
    wave_index,
    brick_count,
    value_weight,
    k_filter,
    mix_weight,
    out_weight,
    norm_gain,
    up_weight,
    down_weight,
):
    rows, width = features.shape
    groups = lax.axis_size("kvec")
    bricks = lax.axis_size("atom")
    k_shard = wave_index.shape[1]
    hidden = up_weight.shape[1]
    capacity = rows * groups
    z_size = bricks // 2
    piece = k_shard // bricks
    lanes = width // PARTS
    normalizer = 1.0 / math.sqrt(bricks * capacity // 2 * (k_shard * groups))
    vmem = pl.BlockSpec(memory_space=pltpu.VMEM)
    hbm = pl.BlockSpec(memory_space=pl.ANY)
    dma = pltpu.SemaphoreType.DMA
    return pl.pallas_call(
        functools.partial(kernel, groups, bricks, normalizer),
        out_shape=jax.ShapeDtypeStruct((rows, width), f32),
        in_specs=[pl.BlockSpec(memory_space=pltpu.SMEM)] + [vmem] * 4 + [hbm] * 6,
        out_specs=vmem,
        scratch_shapes=[
            pltpu.VMEM((2, k_shard, width), f32),
            pltpu.VMEM((width, width), f32),
            pltpu.VMEM((2, width, width), f32),
            pltpu.VMEM((width, width), f32),
            pltpu.VMEM((width, hidden), f32),
            pltpu.VMEM((hidden, width), f32),
            pltpu.VMEM((groups, 8, rows), bf16),
            pltpu.VMEM((k_shard, rows), f32),
            pltpu.VMEM((rows, k_shard), f32),
            pltpu.VMEM((4, groups, k_shard, rows), bf16),
            pltpu.VMEM((4, groups, rows, k_shard), bf16),
            pltpu.VMEM((PARTS, groups, rows, lanes), f32),
            pltpu.VMEM((PARTS, 2, z_size, 2, piece, lanes), f32),
            pltpu.VMEM((PARTS, z_size, 2, piece, lanes), f32),
            pltpu.VMEM((PARTS, z_size, 2, piece, lanes), f32),
            pltpu.VMEM((PARTS, z_size - 1, 2, piece, lanes), f32),
            pltpu.VMEM((PARTS, 2, piece, lanes), f32),
            pltpu.VMEM((PARTS, 2, z_size, 2, piece, lanes), f32),
            pltpu.VMEM((PARTS, groups - 1, rows, lanes), f32),
            pltpu.VMEM((PARTS, groups - 1, rows, lanes), f32),
            dma((6,)),
            dma((PARTS, groups - 1)),
            dma((PARTS, groups - 1)),
            dma((PARTS,)),
            dma((PARTS,)),
            dma((PARTS, z_size - 1)),
            dma((PARTS, z_size - 1)),
            dma((PARTS, z_size - 1)),
            dma((PARTS, z_size - 1)),
            dma((PARTS, z_size)),
            dma((PARTS, z_size)),
            dma((PARTS, groups - 1)),
            dma((PARTS, groups - 1)),
        ],
        compiler_params=pltpu.CompilerParams(
            collective_id=0, has_side_effects=True, vmem_limit_bytes=56 * 1024 * 1024
        ),
    )(
        brick_count,
        features,
        fractions,
        wave_index,
        norm_gain.reshape(1, width),
        k_filter,
        value_weight,
        mix_weight,
        out_weight,
        up_weight,
        down_weight,
    )


def solution(mesh):
    return jax.shard_map(
        shards,
        mesh=mesh,
        in_specs=(
            P(("atom", "kvec"), None),
            P(None, "atom"),
            P(None, "kvec"),
            P(),
            P(),
            P(None, "kvec", None),
            P(),
            P(),
            P(),
            P(),
            P(),
        ),
        out_specs=P(("atom", "kvec"), None),
        check_vma=False,
    )
```

time: 84.7 us -> 68.8 us (0.81)
  the two profiles are of different devices: /device:TPU:24 before, /device:TPU:27 now
where the time goes in v2:
time: 68.8 us; the launch traced here: 68.6 us
  Pallas kernels  66.9 us (97%)
  local copies, waits for them, and re-layouts  1.77 us (3%)
    pallas_call x1, Pallas kernels, shards(): pl.pallas_call(functools.partial(kernel, groups, bricks, normalizer), out...  66.9 us
    unnamed x1, local copies, waits for them, and re-layouts  1.77 us

profile of v2, /device:TPU:27, one launch (start us, length us, event | category | flops | bytes accessed | tf_op | source)
XLA Modules:
  0.0 68.6 jit_solution(6335536158181523556)
XLA Ops:
  0.0 66.9 %shard_map.109 = f32[384,256]{1,0:T(8,128)} custom-call(s32[8]{0:T(128)} %count_ref.1, f32[384,256]{1,0:T(8,128)} %feat_ref.1, s32[3,1536]{1,0:T(4,128)} %frac_ref.1, s32[3,512]{1,0:T(4,128)} %wave_ref.1, f32[1,256]{1,0:T(1,128)} %bitcast.1, f32[2,512,256]{2,1,0:T(8,128)} %kf_hbm.1, f32[256,256]{1,0:T(8,128)} %vw_hbm.1, f32[2,256,256]{2,1,0:T(8,128)} %mix_hbm.1, ...), custom_call_target="tpu_custom_call" | custom-call | tf_op jit(solution)/shard_map/pallas_call | solution.py:386
  66.9 1.8 %copy.13 = f32[384,256]{1,0:T(8,128)} copy(f32[384,256]{1,0:T(8,128)} %shard_map.109) | data formatting | bytes 786432

commit v3 on v2

--- a/solution.py
+++ b/solution.py
@@ -135,7 +135,33 @@
             device_id_type=MESH,
         )
 
-    for h in range(PARTS):
+    square = groups == 4
+    top, low = pl.ds(0, rows // 2), pl.ds(rows // 2, rows // 2)
+    side = g + 1 - 2 * lax.rem(g, 2)
+    over = lax.rem(g + 2, 4)
+    cross = lax.rem(side + 2, 4)
+
+    def x_hop(h, i):
+        if i < 2:
+            src, slot = feat_ref.at[:, h * lanes : (h + 1) * lanes], xbuf.at[h, g]
+        elif i == 2:
+            src = slot = xbuf.at[h, over, top]
+        else:
+            src = slot = xbuf.at[h, side, low]
+        return pltpu.make_async_remote_copy(
+            src_ref=src,
+            dst_ref=slot,
+            send_sem=x_send.at[h, i],
+            recv_sem=x_recv.at[h, i],
+            device_id={"kvec": over if i % 2 else side},
+            device_id_type=MESH,
+        )
+
+    for h in range(PARTS):
+        if square:
+            x_hop(h, 0).start()
+            x_hop(h, 1).start()
+            continue
         for d in range(1, groups):
             x_copy(h, d).start()
 
@@ -207,13 +233,27 @@
         sacc[h, :, :, 0] = re
         sacc[h, :, :, 1] = im
 
+    def add_block(h, j):
+        re, im = gather_term(xbuf[h, j], j)
+        sacc[h, :, :, 0] += re
+        sacc[h, :, :, 1] += im
+
+    def square_blocks(h):
+        x_hop(h, 0).wait_recv()
+        x_hop(h, 3).start()
+        x_hop(h, 1).wait_recv()
+        x_hop(h, 2).start()
+        add_block(h, side)
+        add_block(h, over)
+        x_hop(h, 2).wait_recv()
+        x_hop(h, 3).wait_recv()
+        add_block(h, cross)
+
     def other_blocks(h):
         def take_block(d, carry):
             j = lax.rem(g + groups - d, groups)
             x_copy(h, d).wait_recv()
-            re, im = gather_term(xbuf[h, j], j)
-            sacc[h, :, :, 0] += re
-            sacc[h, :, :, 1] += im
+            add_block(h, j)
             return carry
 
         lax.fori_loop(1, groups, take_block, 0)
@@ -240,7 +280,7 @@
 
     own_block(0)
     for h in range(PARTS):
-        other_blocks(h)
+        (square_blocks if square else other_blocks)(h)
         pair(h).start()
         if h + 1 < PARTS:
             own_block(h + 1)
@@ -301,6 +341,21 @@
             device_id_type=MESH,
         )
 
+    def m_hop(h, i):
+        half_rows = low if i % 2 else top
+        if i < 2:
+            src, slot = mbuf.at[h, 2, half_rows], gbuf.at[h, 0, half_rows]
+        else:
+            src, slot = mbuf.at[h, i - 2], gbuf.at[h, i - 1]
+        return pltpu.make_async_remote_copy(
+            src_ref=src,
+            dst_ref=slot,
+            send_sem=m_send.at[h, i],
+            recv_sem=m_recv.at[h, i],
+            device_id={"kvec": over if i % 2 else side},
+            device_id_type=MESH,
+        )
+
     out_re = (mm3(u_re, mix_re) - mm3(u_im, mix_im)) * normalizer
     out_im = (mm3(u_re, mix_im) + mm3(u_im, mix_re)) * normalizer
     for h in range(PARTS):
@@ -329,9 +384,27 @@
             m_copy(h, d).start()
             return carry
 
-        lax.fori_loop(1, groups, give_block, 0)
+        if square:
+            mbuf[h, 2] = message(cross)
+            m_hop(h, 0).start()
+            m_hop(h, 1).start()
+            mbuf[h, 0] = message(side)
+            mbuf[h, 1] = message(over)
+            m_hop(h, 1).wait_recv()
+            mbuf[h, 0, low] += gbuf[h, 0, low]
+            m_hop(h, 2).start()
+            m_hop(h, 0).wait_recv()
+            mbuf[h, 1, top] += gbuf[h, 0, top]
+            m_hop(h, 3).start()
+        else:
+            lax.fori_loop(1, groups, give_block, 0)
         owns.append(message(g))
     for h in range(PARTS):
+        if square:
+            m_hop(h, 2).wait_recv()
+            m_hop(h, 3).wait_recv()
+            owns[h] = owns[h] + gbuf[h, 1] + gbuf[h, 2]
+            continue
         for d in range(1, groups):
             m_copy(h, d).wait_recv()
             owns[h] = owns[h] + gbuf[h, d - 1]
@@ -348,8 +421,12 @@
     for h in range(PARTS):
         pair(h).wait_send()
         for d in range(1, groups):
-            x_copy(h, d).wait_send()
-            m_copy(h, d).wait_send()
+            if not square:
+                x_copy(h, d).wait_send()
+                m_copy(h, d).wait_send()
+        for i in range(4 if square else 0):
+            x_hop(h, i).wait_send()
+            m_hop(h, i).wait_send()
         for d in range(1, z_size):
             r_copy(h, d).wait_send()
             t_copy(h, d).wait_send()
@@ -410,8 +487,8 @@
             pltpu.VMEM((PARTS, groups - 1, rows, lanes), f32),
             pltpu.VMEM((PARTS, groups - 1, rows, lanes), f32),
             dma((6,)),
-            dma((PARTS, groups - 1)),
-            dma((PARTS, groups - 1)),
+            dma((PARTS, max(groups - 1, 4))),
+            dma((PARTS, max(groups - 1, 4))),
             dma((PARTS,)),
             dma((PARTS,)),
             dma((PARTS, z_size - 1)),
@@ -420,8 +497,8 @@
             dma((PARTS, z_size - 1)),
             dma((PARTS, z_size)),
             dma((PARTS, z_size)),
-            dma((PARTS, groups - 1)),
-            dma((PARTS, groups - 1)),
+            dma((PARTS, max(groups - 1, 4))),
+            dma((PARTS, max(groups - 1, 4))),
         ],
         compiler_params=pltpu.CompilerParams(
             collective_id=0, has_side_effects=True, vmem_limit_bytes=56 * 1024 * 1024

time: 68.8 us -> 66.8 us (0.971)
  the two profiles are of different devices: /device:TPU:27 before, /device:TPU:24 now
where the time goes in v3:
time: 66.8 us; the launch traced here: 66.6 us
  Pallas kernels  64.8 us (97%)
  local copies, waits for them, and re-layouts  1.77 us (3%)
    pallas_call x1, Pallas kernels, shards(): pl.pallas_call(functools.partial(kernel, groups, bricks, normalizer), out...  64.8 us
    unnamed x1, local copies, waits for them, and re-layouts  1.77 us

profile of v3, /device:TPU:24, one launch (start us, length us, event | category | flops | bytes accessed | tf_op | source)
XLA Modules:
  0.0 66.6 jit_solution(18154945421482671339)
XLA Ops:
  0.0 64.8 %shard_map.109 = f32[384,256]{1,0:T(8,128)} custom-call(s32[8]{0:T(128)} %count_ref.1, f32[384,256]{1,0:T(8,128)} %feat_ref.1, s32[3,1536]{1,0:T(4,128)} %frac_ref.1, s32[3,512]{1,0:T(4,128)} %wave_ref.1, f32[1,256]{1,0:T(1,128)} %bitcast.1, f32[2,512,256]{2,1,0:T(8,128)} %kf_hbm.1, f32[256,256]{1,0:T(8,128)} %vw_hbm.1, f32[2,256,256]{2,1,0:T(8,128)} %mix_hbm.1, ...), custom_call_target="tpu_custom_call" | custom-call | tf_op jit(solution)/shard_map/pallas_call | solution.py:463
  64.8 1.8 %copy.13 = f32[384,256]{1,0:T(8,128)} copy(f32[384,256]{1,0:T(8,128)} %shard_map.109) | data formatting | bytes 786432

commit v4 on v3

--- a/solution.py
+++ b/solution.py
@@ -238,13 +238,19 @@
         sacc[h, :, :, 0] += re
         sacc[h, :, :, 1] += im
 
-    def square_blocks(h):
+    def relay(h):
         x_hop(h, 0).wait_recv()
         x_hop(h, 3).start()
         x_hop(h, 1).wait_recv()
         x_hop(h, 2).start()
+
+    def square_blocks(h):
+        if h == 0:
+            relay(0)
         add_block(h, side)
         add_block(h, over)
+        if h + 1 < PARTS:
+            relay(h + 1)
         x_hop(h, 2).wait_recv()
         x_hop(h, 3).wait_recv()
         add_block(h, cross)
@@ -308,8 +314,9 @@
     at = pl.multiple_of(c * half + z * piece, piece)
     k_re = kf[0, pl.ds(at, piece), :]
     k_im = kf[1, pl.ds(at, piece), :]
-    u_re = split(sre * k_re - sim * k_im)
-    u_im = split(sre * k_im + sim * k_re)
+    u_all = split(
+        jnp.concatenate([sre * k_re - sim * k_im, sre * k_im + sim * k_re], axis=0)
+    )
 
     def t_copy(h, d):
         return pltpu.make_async_remote_copy(
@@ -356,8 +363,10 @@
             device_id_type=MESH,
         )
 
-    out_re = (mm3(u_re, mix_re) - mm3(u_im, mix_im)) * normalizer
-    out_im = (mm3(u_re, mix_im) + mm3(u_im, mix_re)) * normalizer
+    by_re = mm3(u_all, mix_re)
+    by_im = mm3(u_all, mix_im)
+    out_re = (by_re[:piece] - by_im[piece:]) * normalizer
+    out_im = (by_im[:piece] + by_re[piece:]) * normalizer
     for h in range(PARTS):
         tsl[h, 0] = out_re[:, h * lanes : (h + 1) * lanes]
         tsl[h, 1] = out_im[:, h * lanes : (h + 1) * lanes]

time: 66.8 us -> 67.7 us (1.013)
  Pallas kernels: 64.8 us -> 65.7 us
    pallas_call x1, Pallas kernels: 64.8 us -> 65.7 us  [shards(): pl.pallas_call(functools.partial(kernel, groups, bricks, normalizer), out...]
where the time goes in v4:
time: 67.7 us; the launch traced here: 67.5 us
  Pallas kernels  65.7 us (97%)
  local copies, waits for them, and re-layouts  1.77 us (3%)
    pallas_call x1, Pallas kernels, shards(): pl.pallas_call(functools.partial(kernel, groups, bricks, normalizer), out...  65.7 us
    unnamed x1, local copies, waits for them, and re-layouts  1.77 us

profile of v4, /device:TPU:24, one launch (start us, length us, event | category | flops | bytes accessed | tf_op | source)
XLA Modules:
  0.0 67.5 jit_solution(15131801005030673354)
XLA Ops:
  0.0 65.7 %shard_map.109 = f32[384,256]{1,0:T(8,128)} custom-call(s32[8]{0:T(128)} %count_ref.1, f32[384,256]{1,0:T(8,128)} %feat_ref.1, s32[3,1536]{1,0:T(4,128)} %frac_ref.1, s32[3,512]{1,0:T(4,128)} %wave_ref.1, f32[1,256]{1,0:T(1,128)} %bitcast.1, f32[2,512,256]{2,1,0:T(8,128)} %kf_hbm.1, f32[256,256]{1,0:T(8,128)} %vw_hbm.1, f32[2,256,256]{2,1,0:T(8,128)} %mix_hbm.1, ...), custom_call_target="tpu_custom_call" | custom-call | tf_op jit(solution)/shard_map/pallas_call | solution.py:472
  65.7 1.8 %copy.13 = f32[384,256]{1,0:T(8,128)} copy(f32[384,256]{1,0:T(8,128)} %shard_map.109) | data formatting | bytes 786432
